TPU v7x, 512 devices: a whole 4x8x8 slice. The times are simulated.
512 devices in a mesh: frame: 512 (over y, z, x, core).
Axes of the slice: x: 4, y: 8, z: 8, core: 2. Of those that a mesh axis runs over, the one named last changes fastest.
Arguments:
- tokens: bfloat16 [786432, 128], P('frame'), may hold values from -8 to 8
- fine_map: bfloat16 [24576, 128, 128], P('frame'), may hold values from -8 to 8
- matches: int32 [512, 2, 2, 512], P('frame'), may hold values from 0 to 1535
- subcells: int32 [512, 2, 2, 512], P('frame'), may hold values from 0 to 3
- counts: int32 [512, 2], P('frame'), may hold values from 64 to 512, as said below
Outputs:
- confidence: float32 [512, 2, 512], P('frame')
- offsets: float32 [512, 2, 2, 512], P('frame')
Inputs may be any that keep to these rules, and one draw needn't show every extreme that they name: `counts`: for each round some frame has exactly 512 valid slots; slots at or beyond the count are ignored.
All inputs are finite; a program needn't handle non-finite values.
Results may differ from a plain program's by a relative error of at most 0.0003.
Values may be sent and summed in bfloat16 or wider, within the bound.
A program may use at most 64 MiB of HBM per device.

v0:
```python
import math

import jax
import jax.numpy as jnp
from jax import lax
from jax.sharding import PartitionSpec as P

NEG_LARGE = -1e30


def from_partner(shard, axis, stride):
    return lax.ppermute(shard, axis, [(i, i ^ 1 << stride) for i in range(lax.axis_size(axis))])


def fetch_partner(tokens, bit):
    return from_partner(tokens, "frame", bit)


def crop_tiles(flat_map, cells, subs, height_fine, width_fine):
    cell_y = 2 * (cells // (width_fine // 2)) + subs // 2
    cell_x = 2 * (cells % (width_fine // 2)) + subs % 2
    spots = jnp.arange(25, dtype=jnp.int32)
    delta_y = spots // 5 - 2
    delta_x = spots % 5 - 2
    near_y = cell_y[:, None] + delta_y[None, :]
    near_x = cell_x[:, None] + delta_x[None, :]
    inside = (near_y >= 0) & (near_y < height_fine) & (near_x >= 0) & (near_x < width_fine)
    index = jnp.clip(near_y, 0, height_fine - 1) * width_fine + jnp.clip(near_x, 0, width_fine - 1)
    return flat_map[index] * inside[:, :, None].astype(flat_map.dtype)


def fine_offsets(tiles, query):
    heat = jnp.einsum("mjc,mc->mj", tiles, query, preferred_element_type=jnp.float32) * tiles.shape[
        -1
    ] ** (-0.5)
    heat = heat - jnp.max(heat, axis=1, keepdims=True)
    expo = jnp.exp(heat)
    weight = expo / jnp.sum(expo, axis=1, keepdims=True)
    spots = jnp.arange(25, dtype=jnp.int32)
    delta_y = (spots // 5 - 2).astype(jnp.float32)
    delta_x = (spots % 5 - 2).astype(jnp.float32)
    return jnp.stack(
        [jnp.sum(weight * delta_x[None, :], axis=1), jnp.sum(weight * delta_y[None, :], axis=1)]
    )


def body(tokens, fine_map, matches, subcells, counts):
    frames = lax.axis_size("frame")
    me_index = lax.axis_index("frame")
    top = frames.bit_length() - 1
    rounds = matches.shape[1]
    slots = matches.shape[3]
    tok_count, width = tokens.shape
    half = tok_count // 2
    scale = 10.0 / width
    height_fine, width_fine, fine_width = fine_map.shape
    flat_map = fine_map.reshape(height_fine * width_fine, fine_width)
    block = math.gcd(tok_count, 512)
    bits = [top - 1 - rnd for rnd in range(rounds)]
    fetched = []
    conf_rounds = []
    offset_rounds = []
    for rnd in range(rounds):
        bit = bits[rnd]
        partner = fetch_partner(tokens, bit)
        is_low = jnp.bitwise_and(jnp.right_shift(me_index, bit), 1) == 0
        low_tokens = jnp.where(is_low, tokens, partner)
        high_source = jnp.where(is_low, partner, tokens)
        high_half = lax.dynamic_slice_in_dim(
            high_source, jnp.where(is_low, 0, half).astype(jnp.int32), half, 0
        )

        def score_block(carry, rows_block):
            col_max, col_sum = carry
            scores = (
                lax.dot_general(
                    rows_block,
                    high_half,
                    (((1,), (1,)), ((), ())),
                    preferred_element_type=jnp.float32,
                )
                * scale
            )
            row_max = jnp.max(scores, axis=1)
            row_sum = jnp.sum(jnp.exp(scores - row_max[:, None]), axis=1)
            blk_max = jnp.max(scores, axis=0)
            blk_sum = jnp.sum(jnp.exp(scores - blk_max[None, :]), axis=0)
            new_max = jnp.maximum(col_max, blk_max)
            new_sum = col_sum * jnp.exp(col_max - new_max) + blk_sum * jnp.exp(blk_max - new_max)
            return ((new_max, new_sum), (row_max, row_sum))

        start = (jnp.full((half,), NEG_LARGE, jnp.float32), jnp.zeros((half,), jnp.float32))
        (col_max, col_sum), (row_max, row_sum) = lax.scan(
            score_block, start, low_tokens.reshape(tok_count // block, block, width)
        )
        empty_max = jnp.full((half,), NEG_LARGE, jnp.float32)
        empty_sum = jnp.zeros((half,), jnp.float32)
        high_max = jnp.where(
            is_low, jnp.concatenate([col_max, empty_max]), jnp.concatenate([empty_max, col_max])
        )
        high_sum = jnp.where(
            is_low, jnp.concatenate([col_sum, empty_sum]), jnp.concatenate([empty_sum, col_sum])
        )
        send_max = jnp.concatenate([row_max.reshape(tok_count), high_max])
        send_sum = jnp.concatenate([row_sum.reshape(tok_count), high_sum])
        got_max, got_sum = from_partner((send_max, send_sum), "frame", bit)
        both_max = jnp.maximum(send_max, got_max)
        both_sum = send_sum * jnp.exp(send_max - both_max) + got_sum * jnp.exp(got_max - both_max)
        merged = both_max + jnp.log(both_sum)
        own_lse = jnp.where(is_low, merged[:tok_count], merged[tok_count:])
        far_lse = jnp.where(is_low, merged[tok_count:], merged[:tok_count])
        own_cells = matches[0, rnd, 0]
        far_cells = matches[0, rnd, 1]
        own_rows = tokens[own_cells].astype(jnp.float32)
        far_rows = partner[far_cells].astype(jnp.float32)
        pair_score = jnp.sum(own_rows * far_rows, axis=1) * scale
        conf = (
            2.0 * pair_score - own_lse[own_cells] - far_lse[far_cells] + 2.0 * math.log(tok_count)
        )
        valid = jnp.arange(slots, dtype=jnp.int32) < counts[0, rnd]
        own_sub = subcells[0, rnd, 0]
        cell_y = 2 * (own_cells // (width_fine // 2)) + own_sub // 2
        cell_x = 2 * (own_cells % (width_fine // 2)) + own_sub % 2
        query = flat_map[cell_y * width_fine + cell_x]
        request = jnp.stack([far_cells, subcells[0, rnd, 1]])
        asked = from_partner(request, "frame", bit)
        local_tiles = crop_tiles(flat_map, asked[0], asked[1], height_fine, width_fine)
        far_tiles = from_partner(local_tiles, "frame", bit)
        offs = fine_offsets(far_tiles, query)
        conf_rounds.append(jnp.where(valid, conf, 0.0))
        offset_rounds.append(jnp.where(valid[None, :], offs, 0.0))
    return (jnp.stack(conf_rounds)[None], jnp.stack(offset_rounds)[None])


def solution(mesh):
    return jax.shard_map(
        body,
        mesh=mesh,
        in_specs=(
            P("frame", None),
            P("frame", None, None),
            P("frame", None, None, None),
            P("frame", None, None, None),
            P("frame", None),
        ),
        out_specs=(P("frame", None, None), P("frame", None, None, None)),
        check_vma=False,
    )
```

profile of v0, /device:TPU:1, one launch (start us, length us, event | category | flops | bytes accessed | tf_op | source)
XLA Modules:
  0.0 394.0 jit_solution(4135551173665428255)
XLA Ops:
  0.7 8.4 %collective-permute-start = (bf16[1536,128]{1,0:T(8,128)(2,1)}, bf16[1536,128]{1,0:T(8,128)(2,1)S(1)}, u32[]{:S(2)}, u32[]{:S(2)}) collective-permute-start(bf16[1536,128]{1,0:T(8,128)(2,1)} %param.9), channel_id=1, source_target_pairs={{0,256},{1,257},{2,258},{3,259},{4,260},{5,261},{6,262},{7,263},{8... | collective-permute-start | bytes 1179656 | tf_op jit(solution)/shard_map/ppermute | solution.py:12
  9.1 2.4 collective-permute-start.3
  11.5 0.8 slice_bitcast_fusion.1
  12.3 3.5 collective-permute-start.6
  15.8 2.1 collective-permute-start.8
  18.0 0.9 compare_select_fusion.3
  19.4 1.3 fusion.58
  20.8 1.1 iota_compare_fusion.1
  23.1 1.2 iota_compare_fusion
  24.3 1.9 gather_fusion.9
  26.2 1.9 gather_fusion.11
  28.1 2.7 gather_fusion
  30.8 1.9 gather_fusion.4
  32.7 1.5 collective-permute-done.6
  34.2 10.9 %collective-permute-done.8 = s32[2,512]{1,0:T(2,128)S(1)} collective-permute-done((s32[2,512]{1,0:T(2,128)S(1)}, s32[2,512]{1,0:T(2,128)S(1)}, u32[]{:S(2)}, u32[]{:S(2)}) %collective-permute-start.8) | collective-permute-done | bytes 4128 | tf_op jit(solution)/shard_map/ppermute | solution.py:12
  45.9 26.3 %gather_fusion.8 = bf16[12800,128]{1,0:T(8,128)(2,1)} fusion(bf16[6144,128]{1,0:T(8,128)(2,1)S(1)} %bitcast.165, s32[13312]{0:T(1024)S(1)} %pad_clamp_fusion.1), kind=kCustom, calls=%fused_computation.8 | custom fusion | bytes 6604800 | tf_op jit(solution)/shard_map/gather | solution.py:29
  72.2 6.5 %reshape.1394 = bf16[512,25,128]{2,1,0:T(8,128)(2,1)} reshape(bf16[12800,128]{1,0:T(8,128)(2,1)} %gather_fusion.8) | data formatting | bytes 6553600 | tf_op jit(solution)/shard_map/gather | solution.py:29
  78.9 5.0 %broadcast_multiply_fusion.1 = bf16[512,25,128]{2,1,0:T(8,128)(2,1)S(1)} fusion(bf16[512,25,128]{2,1,0:T(8,128)(2,1)} %reshape.1394, bf16[512,25]{1,0:T(8,128)(2,1)S(1)} %copy.11), kind=kLoop, calls=%fused_computation.35 | loop fusion | flops 1638400 | bytes 6579200 | tf_op jit(solution)/shard_map/mul | solution.py:29
  83.9 3.1 copy.12
  86.9 4.4 %collective-permute-start.7 = (bf16[512,25,128]{2,0,1:T(8,128)(2,1)}, bf16[512,25,128]{2,0,1:T(8,128)(2,1)}, u32[]{:S(2)}, u32[]{:S(2)}) collective-permute-start(bf16[512,25,128]{2,0,1:T(8,128)(2,1)} %copy.12), channel_id=1, source_target_pairs={{0,256},{1,257},{2,258},{3,259},{4,260},{5,261},{6,262},{7,263},{8... | collective-permute-start | bytes 9830408 | tf_op jit(solution)/shard_map/ppermute | solution.py:12
  91.6 26.3 %gather_fusion.10 = bf16[12800,128]{1,0:T(8,128)(2,1)} fusion(bf16[6144,128]{1,0:T(8,128)(2,1)S(1)} %bitcast.167, s32[13312]{0:T(1024)S(1)} %pad_clamp_fusion), kind=kCustom, calls=%fused_computation.10 | custom fusion | bytes 6604800 | tf_op jit(solution)/shard_map/gather | solution.py:29
  117.9 6.5 %reshape.1410 = bf16[512,25,128]{2,1,0:T(8,128)(2,1)} reshape(bf16[12800,128]{1,0:T(8,128)(2,1)} %gather_fusion.10) | data formatting | bytes 6553600 | tf_op jit(solution)/shard_map/gather | solution.py:29
  124.6 5.0 %broadcast_multiply_fusion = bf16[512,25,128]{2,1,0:T(8,128)(2,1)S(1)} fusion(bf16[512,25,128]{2,1,0:T(8,128)(2,1)} %reshape.1410, bf16[512,25]{1,0:T(8,128)(2,1)S(1)} %copy.13), kind=kLoop, calls=%fused_computation.34 | loop fusion | flops 1638400 | bytes 6579200 | tf_op jit(solution)/shard_map/mul | solution.py:29
  129.6 3.1 copy.14
  132.7 1.9 collective-permute-start.9
  134.6 0.8 broadcast_select_fusion.1
  135.6 6.1 %while.34 = (s32[]{:T(128)}, f32[768]{0:T(1024)S(1)}, f32[768]{0:T(1024)S(1)}, f32[3,512]{1,0:T(4,128)S(1)}, f32[3,512]{1,0:T(4,128)S(1)}, /*index=5*/bf16[3,512...) while((s32[]{:T(128)}, f32[768]{0:T(1024)S(1)}, f32[768]{0:T(1024)S(1)}, ...), condition=%wide.region_6.7_spmd.clone, body=%wide.region_1.6_spmd.clone.sunk | while | flops 103419392 | bytes 3516015 | solution.py:93
  135.6 1.4 fusion.68
  137.6 1.4 fusion.68
  139.7 1.4 fusion.68
  141.8 4.8 %collective-permute-start.1 = (f32[3072]{0:T(1024)S(1)}, f32[3072]{0:T(1024)}, u32[]{:S(2)}, u32[]{:S(2)}) collective-permute-start(f32[3072]{0:T(1024)S(1)} %pad_maximum_fusion), channel_id=1, source_target_pairs={{0,256},{1,257},{2,258},{3,259},{4,260},{5,261},{6,262},{7,263},{8... | collective-permute-start | bytes 36872 | tf_op jit(solution)/shard_map/ppermute | solution.py:12
  146.6 4.4 %collective-permute-start.2 = (f32[3072]{0:T(1024)S(1)}, f32[3072]{0:T(1024)}, u32[]{:S(2)}, u32[]{:S(2)}) collective-permute-start(f32[3072]{0:T(1024)S(1)} %pad_maximum_fusion.1), channel_id=1, source_target_pairs={{0,256},{1,257},{2,258},{3,259},{4,260},{5,261},{6,262},{7,263},{8... | collective-permute-start | bytes 36872 | tf_op jit(solution)/shard_map/ppermute | solution.py:12
  151.1 3.4 while.35
  154.6 4.4 %collective-permute-start.4 = (f32[3072]{0:T(1024)S(1)}, f32[3072]{0:T(1024)S(1)}, u32[]{:S(2)}, u32[]{:S(2)}) collective-permute-start(f32[3072]{0:T(1024)S(1)} %pad_maximum_fusion.2), channel_id=1, source_target_pairs={{0,128},{1,129},{2,130},{3,131},{4,132},{5,133},{6,134},{7,135},{8... | collective-permute-start | bytes 36872 | tf_op jit(solution)/shard_map/ppermute | solution.py:12
  159.0 1.3 gather_fusion.1
  160.4 1.3 gather_fusion.5
  162.1 144.5 %collective-permute-done.1 = f32[3072]{0:T(1024)} collective-permute-done((f32[3072]{0:T(1024)S(1)}, f32[3072]{0:T(1024)}, u32[]{:S(2)}, u32[]{:S(2)}) %collective-permute-start.1) | collective-permute-done | bytes 12320 | tf_op jit(solution)/shard_map/ppermute | solution.py:12
  306.6 1.9 collective-permute-start.5
  308.5 0.8 log_add_fusion.1
  309.3 3.1 gather_fusion.2
  312.5 3.1 gather_fusion.3
  315.6 60.2 %collective-permute-done.4 = f32[3072]{0:T(1024)S(1)} collective-permute-done((f32[3072]{0:T(1024)S(1)}, f32[3072]{0:T(1024)S(1)}, u32[]{:S(2)}, u32[]{:S(2)}) %collective-permute-start.4) | collective-permute-done | bytes 12320 | tf_op jit(solution)/shard_map/ppermute | solution.py:12
  376.1 3.1 gather_fusion.6
  379.3 3.1 gather_fusion.7
  382.4 1.2 compare_select_fusion.6
  384.3 4.2 %fusion.10 = f32[512,1,25]{2,1,0:T(1,128)S(1)} fusion(bf16[512,25,128]{2,0,1:T(8,128)(2,1)} %collective-permute-done.7, bf16[512,128,1]{1,0,2:T(8,128)(2,1)S(1)} %bitcast.176), kind=kOutput, calls=%fused_computation.32 | convolution fusion | flops 3276800 | bytes 3459072 | tf_op jit(solution)/shard_map/mjc,mc->mj/dot_general | solution.py:33
  388.8 4.2 %fusion.8 = f32[512,1,25]{2,1,0:T(1,128)S(1)} fusion(bf16[512,25,128]{2,0,1:T(8,128)(2,1)} %collective-permute-done.9, bf16[512,128,1]{1,0,2:T(8,128)(2,1)S(1)} %bitcast.175), kind=kOutput, calls=%fused_computation.30 | convolution fusion | flops 3276800 | bytes 3459072 | tf_op jit(solution)/shard_map/mjc,mc->mj/dot_general | solution.py:33
  393.4 0.6 maximum_bitcast_fusion
  (125 shorter events, 10.4 us)
Async XLA Ops:
  0.6 23.7 %copy-start = (bf16[48,128,128]{2,1,0:T(8,128)(2,1)S(1)}, bf16[48,128,128]{2,1,0:T(8,128)(2,1)}, u32[]{:S(2)}) copy-start(bf16[48,128,128]{2,1,0:T(8,128)(2,1)} %param.10) | copy-start | bytes 4718596
  0.6 30.2 %copy-start.1 = (bf16[1536,128]{1,0:T(8,128)(2,1)S(1)}, bf16[1536,128]{1,0:T(8,128)(2,1)}, u32[]{:S(2)}) copy-start(bf16[1536,128]{1,0:T(8,128)(2,1)} %param.9) | copy-start | bytes 1179652
  0.7 134.0 %collective-permute-start = (bf16[1536,128]{1,0:T(8,128)(2,1)}, bf16[1536,128]{1,0:T(8,128)(2,1)S(1)}, u32[]{:S(2)}, u32[]{:S(2)}) collective-permute-start(bf16[1536,128]{1,0:T(8,128)(2,1)} %param.9), channel_id=1, source_target_pairs={{0,256},{1,257},{2,258},{3,259},{4,260},{5,261},{6,262},{7,263},{8... | collective-permute-start | bytes 1179656 | tf_op jit(solution)/shard_map/ppermute | solution.py:12
  9.1 125.6 %collective-permute-start.3 = (bf16[1536,128]{1,0:T(8,128)(2,1)}, bf16[1536,128]{1,0:T(8,128)(2,1)S(1)}, u32[]{:S(2)}, u32[]{:S(2)}) collective-permute-start(bf16[1536,128]{1,0:T(8,128)(2,1)} %param.9), channel_id=1, source_target_pairs={{0,128},{1,129},{2,130},{3,131},{4,132},{5,133},{6,134},{7,135},{8... | collective-permute-start | bytes 1179656 | tf_op jit(solution)/shard_map/ppermute | solution.py:12
  12.3 21.9 %collective-permute-start.6 = (s32[2,512]{1,0:T(2,128)S(1)}, s32[2,512]{1,0:T(2,128)S(1)}, u32[]{:S(2)}, u32[]{:S(2)}) collective-permute-start(s32[2,512]{1,0:T(2,128)S(1)} %pad_add_fusion), channel_id=1, source_target_pairs={{0,256},{1,257},{2,258},{3,259},{4,260},{5,261},{6,262},{7,263},{8... | collective-permute-start | bytes 12296 | tf_op jit(solution)/shard_map/ppermute | solution.py:12
  15.8 29.3 %collective-permute-start.8 = (s32[2,512]{1,0:T(2,128)S(1)}, s32[2,512]{1,0:T(2,128)S(1)}, u32[]{:S(2)}, u32[]{:S(2)}) collective-permute-start(s32[2,512]{1,0:T(2,128)S(1)} %pad_add_fusion.1), channel_id=1, source_target_pairs={{0,128},{1,129},{2,130},{3,131},{4,132},{5,133},{6,134},{7,135},{8... | collective-permute-start | bytes 12296 | tf_op jit(solution)/shard_map/ppermute | solution.py:12
  21.9 12.3 %copy-start.10 = (s32[1024]{0:T(1024)}, s32[1024]{0:T(1024)S(1)}, u32[]{:S(2)}) copy-start(s32[1024]{0:T(1024)S(1)} %pad_clamp_fusion.7) | copy-start | bytes 12292
  22.5 11.7 %copy-start.7 = (s32[1024]{0:T(1024)}, s32[1024]{0:T(1024)S(1)}, u32[]{:S(2)}) copy-start(s32[1024]{0:T(1024)S(1)} %pad_clamp_fusion.5) | copy-start | bytes 12292
  86.9 297.3 %collective-permute-start.7 = (bf16[512,25,128]{2,0,1:T(8,128)(2,1)}, bf16[512,25,128]{2,0,1:T(8,128)(2,1)}, u32[]{:S(2)}, u32[]{:S(2)}) collective-permute-start(bf16[512,25,128]{2,0,1:T(8,128)(2,1)} %copy.12), channel_id=1, source_target_pairs={{0,256},{1,257},{2,258},{3,259},{4,260},{5,261},{6,262},{7,263},{8... | collective-permute-start | bytes 9830408 | tf_op jit(solution)/shard_map/ppermute | solution.py:12
  132.7 256.0 %collective-permute-start.9 = (bf16[512,25,128]{2,0,1:T(8,128)(2,1)}, bf16[512,25,128]{2,0,1:T(8,128)(2,1)}, u32[]{:S(2)}, u32[]{:S(2)}) collective-permute-start(bf16[512,25,128]{2,0,1:T(8,128)(2,1)} %copy.14), channel_id=1, source_target_pairs={{0,128},{1,129},{2,130},{3,131},{4,132},{5,133},{6,134},{7,135},{8... | collective-permute-start | bytes 9830408 | tf_op jit(solution)/shard_map/ppermute | solution.py:12
  141.8 164.8 %collective-permute-start.1 = (f32[3072]{0:T(1024)S(1)}, f32[3072]{0:T(1024)}, u32[]{:S(2)}, u32[]{:S(2)}) collective-permute-start(f32[3072]{0:T(1024)S(1)} %pad_maximum_fusion), channel_id=1, source_target_pairs={{0,256},{1,257},{2,258},{3,259},{4,260},{5,261},{6,262},{7,263},{8... | collective-permute-start | bytes 36872 | tf_op jit(solution)/shard_map/ppermute | solution.py:12
  146.6 161.9 %collective-permute-start.2 = (f32[3072]{0:T(1024)S(1)}, f32[3072]{0:T(1024)}, u32[]{:S(2)}, u32[]{:S(2)}) collective-permute-start(f32[3072]{0:T(1024)S(1)} %pad_maximum_fusion.1), channel_id=1, source_target_pairs={{0,256},{1,257},{2,258},{3,259},{4,260},{5,261},{6,262},{7,263},{8... | collective-permute-start | bytes 36872 | tf_op jit(solution)/shard_map/ppermute | solution.py:12
  151.0 8.0 %copy-start.9 = (s32[1024]{0:T(1024)S(1)}, s32[1024]{0:T(1024)}, u32[]{:S(2)}) copy-start(s32[1024]{0:T(1024)} %pad_clamp_fusion.6) | copy-start | bytes 12292
  151.1 9.3 %copy-start.6 = (s32[1024]{0:T(1024)S(1)}, s32[1024]{0:T(1024)}, u32[]{:S(2)}) copy-start(s32[1024]{0:T(1024)} %pad_clamp_fusion.4) | copy-start | bytes 12292
  151.1 10.7 %copy-start.3 = (bf16[512,128]{1,0:T(8,128)(2,1)S(1)}, bf16[512,128]{1,0:T(8,128)(2,1)}, u32[]{:S(2)}) copy-start(bf16[512,128]{1,0:T(8,128)(2,1)} %gather_fusion) | copy-start | bytes 393220
  151.1 10.9 %copy-start.2 = (bf16[512,128]{1,0:T(8,128)(2,1)S(1)}, bf16[512,128]{1,0:T(8,128)(2,1)}, u32[]{:S(2)}) copy-start(bf16[512,128]{1,0:T(8,128)(2,1)} %gather_fusion.4) | copy-start | bytes 393220
  151.1 158.2 %copy-start.11 = (s32[1024]{0:T(1024)S(1)}, s32[1024]{0:T(1024)}, u32[]{:S(2)}) copy-start(s32[1024]{0:T(1024)} %copy-done.10) | copy-start | bytes 12292
  154.6 221.3 %collective-permute-start.4 = (f32[3072]{0:T(1024)S(1)}, f32[3072]{0:T(1024)S(1)}, u32[]{:S(2)}, u32[]{:S(2)}) collective-permute-start(f32[3072]{0:T(1024)S(1)} %pad_maximum_fusion.2), channel_id=1, source_target_pairs={{0,128},{1,129},{2,130},{3,131},{4,132},{5,133},{6,134},{7,135},{8... | collective-permute-start | bytes 36872 | tf_op jit(solution)/shard_map/ppermute | solution.py:12
  160.4 215.7 %copy-start.8 = (s32[1024]{0:T(1024)S(1)}, s32[1024]{0:T(1024)}, u32[]{:S(2)}) copy-start(s32[1024]{0:T(1024)} %copy-done.7) | copy-start | bytes 12292
  306.6 69.5 %collective-permute-start.5 = (f32[3072]{0:T(1024)S(1)}, f32[3072]{0:T(1024)S(1)}, u32[]{:S(2)}, u32[]{:S(2)}) collective-permute-start(f32[3072]{0:T(1024)S(1)} %pad_maximum_fusion.3), channel_id=1, source_target_pairs={{0,128},{1,129},{2,130},{3,131},{4,132},{5,133},{6,134},{7,135},{8... | collective-permute-start | bytes 36872 | tf_op jit(solution)/shard_map/ppermute | solution.py:12
  312.5 71.8 %copy-start.5 = (bf16[512,128]{1,0:T(8,128)(2,1)S(1)}, bf16[512,128]{1,0:T(8,128)(2,1)}, u32[]{:S(2)}) copy-start(bf16[512,128]{1,0:T(8,128)(2,1)} %gather_fusion.9) | copy-start | bytes 393220
  384.3 4.5 %copy-start.4 = (bf16[512,128]{1,0:T(8,128)(2,1)S(1)}, bf16[512,128]{1,0:T(8,128)(2,1)}, u32[]{:S(2)}) copy-start(bf16[512,128]{1,0:T(8,128)(2,1)} %gather_fusion.11) | copy-start | bytes 393220
  388.7 4.4 %copy-start.12 = (f32[25]{0:T(128)S(1)}, f32[25]{0:T(128)}, u32[]{:S(2)}) copy-start(f32[25]{0:T(128)} %get-tuple-element.220) | copy-start | bytes 304
  388.7 4.4 %copy-start.13 = (f32[25]{0:T(128)S(1)}, f32[25]{0:T(128)}, u32[]{:S(2)}) copy-start(f32[25]{0:T(128)} %get-tuple-element.221) | copy-start | bytes 304
  388.7 4.6 %copy-start.14 = (pred[512]{0:T(512)(128)(4,1)S(1)}, pred[512]{0:T(512)(128)(4,1)}, u32[]{:S(2)}) copy-start(pred[512]{0:T(512)(128)(4,1)} %iota_compare_fusion.1) | copy-start | bytes 1540
  388.8 4.6 %copy-start.15 = (pred[512]{0:T(512)(128)(4,1)S(1)}, pred[512]{0:T(512)(128)(4,1)}, u32[]{:S(2)}) copy-start(pred[512]{0:T(512)(128)(4,1)} %iota_compare_fusion) | copy-start | bytes 1540
where the time goes:
time: 395 us; the launch traced here: 394 us
  waiting for transfers between devices  217 us (55%)
  local copies, waits for them, and re-layouts  99.3 us (25%)
  starting transfers between devices  38.4 us (10%)
  other arithmetic  23.6 us (6%)
  matrix products  13.9 us (4%)
    ppermute x10, waiting for transfers between devices, from_partner(): lax.ppermute(shard, axis, [(i, i ^ 1 << stride) for i in range(lax.axis_s...  217 us
    gather x4, local copies, waits for them, and re-layouts, crop_tiles(): return flat_map[index] * inside[:, :, None].astype(flat_map.dtype)  65.6 us
    ppermute x10, starting transfers between devices, from_partner(): lax.ppermute(shard, axis, [(i, i ^ 1 << stride) for i in range(lax.axis_s...  38.4 us
    mul x2, other arithmetic, crop_tiles(): return flat_map[index] * inside[:, :, None].astype(flat_map.dtype)  10 us
    dot_general x2, matrix products, fine_offsets(): jnp.einsum('mjc,mc->mj', tiles, query, preferred_element_type=jnp.float32)  8.43 us
  transfers between devices with their start and end apart: 10, of which 5 were waited for; matrix products, arithmetic and copies ran while one was open for 33% of the time, Pallas kernels for 0%

commit v1 on v0

v1 whole, which is shorter than its diff:
```python
import math

import jax
import jax.numpy as jnp
from jax import lax
from jax.experimental import pallas as pl
from jax.experimental.pallas import tpu as pltpu
from jax.sharding import PartitionSpec as P

MESH = pl.DeviceIdType.MESH
F32 = jnp.float32
BF16 = jnp.bfloat16
NEG = -1e30
YRING = 8


def kernel(
    devices, tok_hbm, map_hbm, mat_hbm, sub_hbm, cnt_ref, conf_ref, off_ref,
    mapb, mapf, left, right, mleft, mright, mat, sub, pvec, psm, req_out, req_in, qf, q_out, q_in,
    heat, acc, scores, onehot, got_left, got_right, lse_left, lse_right,
    off_out, off_in, conf_out, conf_in, lsem, ssem, rsem,
):
    tok_count, width = tok_hbm.shape
    points = map_hbm.shape[0]
    fine_w = 128
    fine_h = points // fine_w
    slots = mat.shape[2]
    scale = 10.0 / width
    stride = devices // YRING
    me = lax.axis_index("frame")
    row = me // stride
    rest = me % stride
    core = rest % 2
    low = (row // 2) % 2
    home = (row // 4 + low + core + 1) % 2
    near = row + 2 - 4 * low
    opposite = (row + 4) % YRING
    far = (near + 4) % YRING

    def at(yy, cc):
        return (yy * stride + (rest - core) + cc,)

    sibling = at(row, 1 - core)
    near_same, near_other = at(near, core), at(near, 1 - core)
    opp_same, far_other = at(opposite, core), at(far, 1 - core)

    def remote(src, dst, i, dev):
        return pltpu.make_async_remote_copy(
            src_ref=src, dst_ref=dst, send_sem=ssem.at[i], recv_sem=rsem.at[i], device_id=dev, device_id_type=MESH
        )

    map_cp = pltpu.make_async_copy(map_hbm, mapb, lsem.at[0])
    mat_cp = pltpu.make_async_copy(mat_hbm, mat, lsem.at[1])
    sub_cp = pltpu.make_async_copy(sub_hbm, sub, lsem.at[2])
    own_cp = pltpu.make_async_copy(tok_hbm, left, lsem.at[3])
    mat_cp.start()
    sub_cp.start()
    map_cp.start()

    bar = pltpu.get_barrier_semaphore()
    peers = (sibling, near_same, near_other, opp_same, far_other)
    for peer in peers:
        pl.semaphore_signal(bar, inc=1, device_id=peer, device_id_type=MESH)
    pl.semaphore_wait(bar, len(peers))

    tok_a = remote(tok_hbm, left, 0, far_other)
    mat_a = remote(mat_hbm, mleft, 1, far_other)
    tok_b = remote(tok_hbm, right, 2, near_same)
    mat_b = remote(mat_hbm, mright, 3, near_same)
    tok_f = remote(right, right, 2, sibling)
    mat_f = remote(mright, mright, 3, sibling)

    @pl.when(home == 1)
    def _():
        mat_a.start()
        tok_a.start()
        own_cp.start()

    @pl.when(home == 0)
    def _():
        mat_b.start()
        tok_b.start()

    mat_cp.wait()
    sub_cp.wait()
    for rnd in range(2):
        cells, subs = mat[rnd], sub[rnd]
        yy = 2 * (cells >> 6) + (subs >> 1)
        xx = 2 * (cells & 63) + (subs & 1)
        pvec[rnd : rnd + 1, :] = (yy * fine_w + xx)[0:1, :]
        req_out[rnd, 0:1, :] = yy[1:2, :]
        req_out[rnd, 1:2, :] = xx[1:2, :]
    p_cp = pltpu.make_async_copy(pvec, psm, lsem.at[1])
    p_cp.start()
    map_cp.wait()

    @pl.loop(0, points // 256)
    def _(i):
        blk = pl.ds(pl.multiple_of(i * 256, 256), 256)
        mapf[blk, :] = mapb[blk, :].astype(F32)

    p_cp.wait()
    q_cps = []
    for rnd in range(2):

        @pl.loop(0, slots // 8)
        def _(g):
            for s in range(8):
                j = g * 8 + s
                qf[pl.ds(j, 1), :] = mapf[pl.ds(psm[rnd, j], 1), :]

        q_out[rnd] = qf[...].astype(BF16)
        dev = opp_same if rnd == 0 else near_same
        for cp in (remote(req_out.at[rnd], req_in.at[rnd], 4 + rnd, dev), remote(q_out.at[rnd], q_in.at[rnd], 6 + rnd, dev)):
            cp.start()
            q_cps.append(cp)

    @pl.when(home == 1)
    def _():
        mat_b.wait_recv()
        tok_b.wait_recv()
        mat_f.start()
        tok_f.start()
        own_cp.wait()
        mleft[...] = mat[...]

    @pl.when(home == 0)
    def _():
        mat_a.wait_recv()
        tok_a.wait_recv()
        mat_f.wait_recv()
        tok_f.wait_recv()

    def col_lse(rows, cols, out):
        for jb in range(tok_count // 512):

            def dots(i, m8):
                blk = pl.ds(pl.multiple_of(i * 256, 256), 256)
                s = lax.dot_general(
                    rows[blk, :], cols[jb * 512 : (jb + 1) * 512, :], (((1,), (1,)), ((), ())), preferred_element_type=F32
                )
                scores[blk, :] = s
                return jnp.maximum(m8, jnp.max(s.reshape(32, 8, 512), axis=0))

            m8 = lax.fori_loop(0, tok_count // 256, dots, jnp.full((8, 512), NEG, F32))
            top = jnp.max(m8, axis=0, keepdims=True)

            def sums(i, s8):
                s = scores[pl.ds(pl.multiple_of(i * 64, 64), 64), :]
                return s8 + jnp.sum(jnp.exp((s - top) * scale).reshape(8, 8, 512), axis=0)

            s8 = lax.fori_loop(0, tok_count // 64, sums, jnp.zeros((8, 512), F32))
            out[0:1, jb * 512 : (jb + 1) * 512] = top * scale + jnp.log(jnp.sum(s8, axis=0, keepdims=True))

    col_lse(right, left, lse_left)
    col_lse(left, right, lse_right)

    def gather(toks, lse, index, got):
        @pl.loop(0, tok_count // 64)
        def _(i):
            blk = pl.ds(pl.multiple_of(i * 64, 64), 64)
            tt = lax.broadcasted_iota(jnp.int32, (64, 2 * slots), 0) + i * 64
            onehot[blk, :] = jnp.where(tt == index, 1.0, 0.0).astype(BF16)

        v = lse[0:1, :]
        hi = v.astype(BF16)
        mid = (v - hi.astype(F32)).astype(BF16)
        lo = (v - hi.astype(F32) - mid.astype(F32)).astype(BF16)
        pieces = jnp.concatenate([hi.astype(F32), mid.astype(F32), lo.astype(F32), jnp.zeros((13, tok_count), F32)], axis=0)
        got[0:width, :] = lax.dot_general(toks[...], onehot[...], (((0,), (0,)), ((), ())), preferred_element_type=F32)
        got[width : width + 16, :] = jnp.dot(pieces.astype(BF16), onehot[...], preferred_element_type=F32)

    ml, mr = mleft[1 * home], mright[1 * home]
    gather(left, lse_left, jnp.concatenate([ml[0:1, :], mr[1:2, :]], axis=1), got_left)
    gather(right, lse_right, jnp.concatenate([ml[1:2, :], mr[0:1, :]], axis=1), got_right)
    pair = jnp.sum(got_left[0:width, :] * got_right[0:width, :], axis=0, keepdims=True) * scale
    lses = jnp.sum(got_left[width : width + 8, :] + got_right[width : width + 8, :], axis=0, keepdims=True)
    conf = 2.0 * pair - lses + 2.0 * math.log(tok_count)
    conf_out[0] = conf[:, 0:slots]
    conf_out[1] = conf[:, slots:]
    conf_r = remote(conf_out.at[1], conf_in.at[home], 9 - home, at(near, home * core + (1 - home) * (1 - core)))
    conf_l = remote(conf_out.at[0], conf_in.at[0], 10, far_other)
    conf_w0 = remote(conf_out.at[1], conf_in.at[0], 9, near_other)
    conf_w1 = remote(conf_out.at[1], conf_in.at[1], 8, near_same)
    conf_r.start()

    @pl.when(home == 0)
    def _():
        conf_l.start()

    def refine(rnd):
        def dots(i, carry):
            blk = pl.ds(pl.multiple_of(i * 512, 512), 512)
            heat[blk, :] = lax.dot_general(
                mapb[blk, :], q_in[rnd], (((1,), (1,)), ((), ())), preferred_element_type=F32
            )
            return carry

        lax.fori_loop(0, points // 512, dots, 0)

        @pl.loop(0, slots // 128)
        def _(jt):
            lane = pl.ds(pl.multiple_of(jt * 128, 128), 128)
            ylow = jnp.broadcast_to(req_in[rnd, 0:1, lane] - 2, (8, 128))
            xmid = jnp.broadcast_to(req_in[rnd, 1:2, lane], (8, 128))

            @pl.loop(0, 4)
            def _(xb):
                accs = [[jnp.zeros((8, 128), F32) for _ in range(4)] for _ in range(5)]
                for yy in range(fine_h):
                    d = yy - ylow
                    hit = (d >= 0) & (d < 5)
                    for k in range(4):
                        h = heat[pl.ds(pl.multiple_of(yy * fine_w + xb * 32 + k * 8, 8), 8), lane]
                        accs[yy % 5][k] = jnp.where(hit, h, accs[yy % 5][k])
                for r in range(5):
                    for k in range(4):
                        acc[r, pl.ds(pl.multiple_of(xb * 32 + k * 8, 8), 8), lane] = accs[r][k] * (width ** -0.5)

            iota = lax.broadcasted_iota(jnp.int32, (8, 128), 0)
            m8 = jnp.full((8, 128), NEG, F32)
            for xt in range(fine_w // 8):
                dx = iota + xt * 8 - xmid
                inside = (dx >= -2) & (dx <= 2)
                v = acc[0, xt * 8 : xt * 8 + 8, lane]
                for r in range(1, 5):
                    v = jnp.maximum(v, acc[r, xt * 8 : xt * 8 + 8, lane])
                m8 = jnp.maximum(m8, jnp.where(inside, v, NEG))
            x1 = xmid[0:1, :]
            missing = jnp.maximum(2 - x1, 0) + jnp.maximum(x1 - (fine_w - 3), 0)
            top = jnp.max(m8, axis=0, keepdims=True)
            top = jnp.where(missing > 0, jnp.maximum(top, 0.0), top)
            topb = jnp.broadcast_to(top, (8, 128))
            z = [jnp.zeros((8, 128), F32) for _ in range(5)]
            sx = jnp.zeros((8, 128), F32)
            for xt in range(fine_w // 8):
                dx = iota + xt * 8 - xmid
                inside = (dx >= -2) & (dx <= 2)
                tot = jnp.zeros((8, 128), F32)
                for r in range(5):
                    e = jnp.where(inside, jnp.exp(acc[r, xt * 8 : xt * 8 + 8, lane] - topb), 0.0)
                    z[r] = z[r] + e
                    tot = tot + e
                sx = sx + tot * dx.astype(F32)
            sy = jnp.zeros((8, 128), F32)
            tot = jnp.zeros((8, 128), F32)
            for r in range(5):
                t = r - ylow + 50
                dy = t - 5 * ((t * 205) >> 10) - 2
                sy = sy + z[r] * dy.astype(F32)
                tot = tot + z[r]
            tot1 = jnp.sum(tot, axis=0, keepdims=True)
            sx1 = jnp.sum(sx, axis=0, keepdims=True)
            sy1 = jnp.sum(sy, axis=0, keepdims=True)
            zero = jnp.where(missing > 0, jnp.exp(-jnp.maximum(top, 0.0)), 0.0) * 5.0
            gone = jnp.where(x1 == 0, -3.0, 0.0) + jnp.where(x1 == 1, -2.0, 0.0)
            gone = gone + jnp.where(x1 == fine_w - 1, 3.0, 0.0) + jnp.where(x1 == fine_w - 2, 2.0, 0.0)
            tot1 = tot1 + zero * missing.astype(F32)
            sx1 = sx1 + zero * gone
            off_out[rnd, 0:1, lane] = sx1 / tot1
            off_out[rnd, 1:2, lane] = sy1 / tot1

    off_cps = []
    for rnd in range(2):
        q_cps[2 * rnd].wait_recv()
        q_cps[2 * rnd + 1].wait_recv()
        refine(rnd)
        cp = remote(off_out.at[rnd], off_in.at[rnd], 11 + rnd, opp_same if rnd == 0 else near_same)
        cp.start()
        off_cps.append(cp)

    for rnd in range(2):
        off_cps[rnd].wait_recv()
        valid = lax.broadcasted_iota(jnp.int32, (2, slots), 1) < cnt_ref[0, rnd]
        off_ref[rnd] = jnp.where(valid, off_in[rnd], 0.0)

    @pl.when(home == 1)
    def _():
        conf_l.wait_recv()
        conf_in[1] = conf_out[0]

    @pl.when(home == 0)
    def _():
        conf_w0.wait_recv()
        conf_w1.wait_recv()

    for rnd in range(2):
        valid = lax.broadcasted_iota(jnp.int32, (1, slots), 1) < cnt_ref[0, rnd]
        conf_ref[rnd : rnd + 1, :] = jnp.where(valid, conf_in[rnd], 0.0)

    for cp in q_cps + off_cps + [conf_r]:
        cp.wait_send()

    @pl.when(home == 1)
    def _():
        mat_a.wait_send()
        tok_a.wait_send()
        mat_f.wait_send()
        tok_f.wait_send()

    @pl.when(home == 0)
    def _():
        mat_b.wait_send()
        tok_b.wait_send()
        conf_l.wait_send()


def solution(mesh):
    devices = mesh.size

    def body(tokens, fine_map, matches, subcells, counts):
        tok_count, width = tokens.shape
        fine_h, fine_w, _ = fine_map.shape
        points = fine_h * fine_w
        slots = matches.shape[3]
        any_spec = pl.BlockSpec(memory_space=pl.ANY)
        vmem = pltpu.VMEM
        conf, offs = pl.pallas_call(
            lambda *refs: kernel(devices, *refs),
            name="match_refine",
            out_shape=(
                jax.ShapeDtypeStruct((2, slots), F32),
                jax.ShapeDtypeStruct((2, 2, slots), F32),
            ),
            in_specs=[any_spec] * 4 + [pl.BlockSpec(memory_space=pltpu.SMEM)],
            out_specs=(pl.BlockSpec(memory_space=pltpu.VMEM), pl.BlockSpec(memory_space=pltpu.VMEM)),
            scratch_shapes=[
                vmem((points, width), BF16),
                vmem((points, width), F32),
                vmem((tok_count, width), BF16),
                vmem((tok_count, width), BF16),
                vmem((2, 2, slots), jnp.int32),
                vmem((2, 2, slots), jnp.int32),
                vmem((2, 2, slots), jnp.int32),
                vmem((2, 2, slots), jnp.int32),
                vmem((2, slots), jnp.int32),
                pltpu.SMEM((2, slots), jnp.int32),
                vmem((2, 2, slots), jnp.int32),
                vmem((2, 2, slots), jnp.int32),
                vmem((slots, width), F32),
                vmem((2, slots, width), BF16),
                vmem((2, slots, width), BF16),
                vmem((points, slots), F32),
                vmem((5, fine_w, slots), F32),
                vmem((tok_count, 512), F32),
                vmem((tok_count, 2 * slots), BF16),
                vmem((width + 16, 2 * slots), F32),
                vmem((width + 16, 2 * slots), F32),
                vmem((1, tok_count), F32),
                vmem((1, tok_count), F32),
                vmem((2, 2, slots), F32),
                vmem((2, 2, slots), F32),
                vmem((2, 1, slots), F32),
                vmem((2, 1, slots), F32),
                pltpu.SemaphoreType.DMA((4,)),
                pltpu.SemaphoreType.DMA((13,)),
                pltpu.SemaphoreType.DMA((13,)),
            ],
            compiler_params=pltpu.CompilerParams(
                collective_id=0, has_side_effects=True, vmem_limit_bytes=60 * 1024 * 1024
            ),
        )(tokens, fine_map.reshape(points, width), matches[0], subcells[0], counts)
        return conf[None], offs[None]

    return jax.shard_map(
        body,
        mesh=mesh,
        in_specs=(
            P("frame", None),
            P("frame", None, None),
            P("frame", None, None, None),
            P("frame", None, None, None),
            P("frame", None),
        ),
        out_specs=(P("frame", None, None), P("frame", None, None, None)),
        check_vma=False,
    )
```

time: 395 us -> 71.6 us (0.18)
  waiting for transfers between devices: 217 us -> 0 us
  local copies, waits for them, and re-layouts: 99.3 us -> 2.56 us
  Pallas kernels: 0 us -> 68.2 us
  starting transfers between devices: 38.4 us -> 0 us
  other arithmetic: 23.6 us -> 0 us
  matrix products: 13.9 us -> 0 us
    ppermute x10 -> x0, waiting for transfers between devices: 217 us -> none  [from_partner(): lax.ppermute(shard, axis, [(i, i ^ 1 << stride) for i in range(lax.axis_s...]
    gather x14 -> x0, local copies, waits for them, and re-layouts: 89.2 us -> none  [the longest x4 65.6 us: crop_tiles(): return flat_map[index] * inside[:, :, None].astype(flat_map.dtype)]
    pallas_call x0 -> x1, Pallas kernels: none -> 68.2 us  [body(): pl.pallas_call(lambda *refs: kernel(devices, *refs), name='match_refine',...]
    ppermute x10 -> x0, starting transfers between devices: 38.4 us -> none  [from_partner(): lax.ppermute(shard, axis, [(i, i ^ 1 << stride) for i in range(lax.axis_s...]
    dot_general x8 -> x0, matrix products: 13.9 us -> none  [the longest x2 8.43 us: fine_offsets(): jnp.einsum('mjc,mc->mj', tiles, query, preferred_element_type=jnp.float32)]
    mul x2 -> x0, other arithmetic: 10 us -> none  [crop_tiles(): return flat_map[index] * inside[:, :, None].astype(flat_map.dtype)]
    mul x2 -> x0, local copies, waits for them, and re-layouts: 6.17 us -> none  [crop_tiles(): return flat_map[index] * inside[:, :, None].astype(flat_map.dtype)]
  transfers between devices with their start and end apart: 10 -> 0, of which waited for: 5 -> 0; matrix products, arithmetic and copies ran while one was open for 33% -> 0% of each run, Pallas kernels for 0% -> 0%
where the time goes in v1:
time: 71.6 us; the launch traced here: 71.4 us
  Pallas kernels  68.2 us (95%)
  local copies, waits for them, and re-layouts  2.56 us (4%)
    pallas_call x1, Pallas kernels, body(): pl.pallas_call(lambda *refs: kernel(devices, *refs), name='match_refine',...  68.2 us
    unnamed x2, local copies, waits for them, and re-layouts  2.56 us

profile of v1, /device:TPU:1, one launch (start us, length us, event | category | flops | bytes accessed | tf_op | source)
XLA Modules:
  0.0 71.4 jit_solution(6799790039937750014)
XLA Ops:
  0.6 68.2 %match_refine.1 = (f32[2,512]{1,0:T(2,128)}, f32[2,2,512]{2,1,0:T(2,128)}) custom-call(bf16[1536,128]{1,0:T(8,128)(2,1)} %refs_0_.1, bf16[6144,128]{1,0:T(8,128)(2,1)} %bitcast.5, s32[2,2,512]{2,1,0:T(2,128)} %bitcast.6, s32[2,2,512]{2,1,0:T(2,128)} %bitcast.7, s32[1,2]{1,0:T(1,128)} %refs_4_.1), custom_call_target="tpu_custom_call" | custom-call | tf_op jit(solution)/shard_map/match_refine/pallas_call | solution.py:318
  68.8 1.3 %copy.9 = f32[1,2,512]{2,1,0:T(2,128)} copy(f32[1,2,512]{2,1,0:T(2,128)} %bitcast.9) | data formatting | bytes 8192
  70.1 1.3 %copy.10 = f32[1,2,2,512]{3,2,1,0:T(2,128)} copy(f32[1,2,2,512]{3,2,1,0:T(2,128)} %bitcast.8) | data formatting | bytes 16384

commit v2 on v1

v2 whole, which is shorter than its diff:
```python
import math

import jax
import jax.numpy as jnp
from jax import lax
from jax.experimental import pallas as pl
from jax.experimental.pallas import tpu as pltpu
from jax.sharding import PartitionSpec as P

MESH = pl.DeviceIdType.MESH
F32 = jnp.float32
BF16 = jnp.bfloat16
NEG = -1e30
YRING = 8


def kernel(
    devices, tok_hbm, map_hbm, mat_hbm, sub_hbm, res_ref,
    mapb, mapf, left, right, mleft, mright, mat, sub, pvec, psm0, psm1, req_out, req_in, qf, q_out, q_in,
    acc, scores, lse_col, table_l, table_r, index, conf_both,
    off_out, off_in, conf_out, conf_in, lsem, ssem, rsem,
):
    tok_count, width = tok_hbm.shape
    fine_h, fine_w, _ = map_hbm.shape
    points = fine_h * fine_w
    slots = mat.shape[2]
    scale = 10.0 / width
    stride = devices // YRING
    me = lax.axis_index("frame")
    row = me // stride
    rest = me % stride
    core = rest % 2
    low = (row // 2) % 2
    home = (row // 4 + low + core + 1) % 2
    near = row + 2 - 4 * low
    opposite = (row + 4) % YRING
    far = (near + 4) % YRING

    def at(yy, cc):
        return (yy * stride + (rest - core) + cc,)

    sibling = at(row, 1 - core)
    near_same, near_other = at(near, core), at(near, 1 - core)
    opp_same, far_other = at(opposite, core), at(far, 1 - core)

    def remote(src, dst, i, dev):
        return pltpu.make_async_remote_copy(
            src_ref=src, dst_ref=dst, send_sem=ssem.at[i], recv_sem=rsem.at[i], device_id=dev, device_id_type=MESH
        )

    map_cp = pltpu.make_async_copy(map_hbm, mapb, lsem.at[0])
    mat_cp = pltpu.make_async_copy(mat_hbm, mat, lsem.at[1])
    sub_cp = pltpu.make_async_copy(sub_hbm, sub, lsem.at[2])
    own_cp = pltpu.make_async_copy(tok_hbm, left, lsem.at[3])
    mat_cp.start()
    sub_cp.start()
    map_cp.start()

    bar = pltpu.get_barrier_semaphore()
    peers = (sibling, near_same, near_other, opp_same, far_other)
    for peer in peers:
        pl.semaphore_signal(bar, inc=1, device_id=peer, device_id_type=MESH)
    pl.semaphore_wait(bar, len(peers))

    tok_a = remote(tok_hbm, left, 0, far_other)
    mat_a = remote(mat_hbm, mleft, 1, far_other)
    tok_b = remote(tok_hbm, right, 2, near_same)
    mat_b = remote(mat_hbm, mright, 3, near_same)
    tok_f = remote(right, right, 2, sibling)
    mat_f = remote(mright, mright, 3, sibling)

    @pl.when(home == 1)
    def _():
        mat_a.start()
        tok_a.start()
        own_cp.start()

    @pl.when(home == 0)
    def _():
        mat_b.start()
        tok_b.start()

    mat_cp.wait()
    sub_cp.wait()
    for rnd in range(2):
        cells, subs = mat[rnd], sub[rnd]
        yy = 2 * (cells >> 6) + (subs >> 1)
        xx = 2 * (cells & 63) + (subs & 1)
        pvec[rnd] = (yy * fine_w + xx)[0:1, :]
        req_out[rnd, 0:1, :] = yy[1:2, :]
        req_out[rnd, 1:2, :] = xx[1:2, :]
    p_cps = [
        pltpu.make_async_copy(pvec.at[0], psm0, lsem.at[1]),
        pltpu.make_async_copy(pvec.at[1], psm1, lsem.at[2]),
    ]
    for cp in p_cps:
        cp.start()
    map_cp.wait()

    @pl.loop(0, fine_h // 2)
    def _(i):
        rows = mapb[pl.ds(2 * i, 2)].reshape(2 * fine_w, width)
        mapf[pl.ds(pl.multiple_of(i * 2 * fine_w, 2 * fine_w), 2 * fine_w), :] = rows.astype(F32)

    for cp in p_cps:
        cp.wait()
    for rnd in range(2):

        @pl.loop(0, slots // 16)
        def _(g):
            for s in range(16):
                j = g * 16 + s
                qf[pl.ds(j, 1), :] = mapf[pl.ds((psm0, psm1)[rnd][0, j], 1), :]

        q_out[rnd] = qf[...].astype(BF16)

    @pl.when(home == 1)
    def _():
        tok_a.wait_send()

    @pl.when(home == 0)
    def _():
        tok_b.wait_send()

    q_cps = []
    for rnd in range(2):
        dev = opp_same if rnd == 0 else near_same
        for cp in (remote(req_out.at[rnd], req_in.at[rnd], 4 + rnd, dev), remote(q_out.at[rnd], q_in.at[rnd], 6 + rnd, dev)):
            cp.start()
            q_cps.append(cp)

    @pl.when(home == 1)
    def _():
        mat_b.wait_recv()
        tok_b.wait_recv()
        mat_f.start()
        tok_f.start()
        own_cp.wait()
        mleft[...] = mat[...]

    @pl.when(home == 0)
    def _():
        mat_a.wait_recv()
        tok_a.wait_recv()
        mat_f.wait_recv()
        tok_f.wait_recv()

    unit = scale * math.log2(math.e)
    block = 256

    def score_rows(i, m8):
        blk = pl.ds(pl.multiple_of(i * block, block), block)
        s = lax.dot_general(left[blk, :], right[...], (((1,), (1,)), ((), ())), preferred_element_type=F32) * unit
        scores[blk, :] = s
        m8 = jnp.maximum(m8, jnp.max(s.reshape(block // 8, 8, tok_count), axis=0))
        part = s[:, 0:128]
        for c in range(128, tok_count, 128):
            part = jnp.maximum(part, s[:, c : c + 128])
        top = jnp.max(part, axis=1, keepdims=True)
        tot = jnp.zeros((block, 128), F32)
        for c in range(0, tok_count, 128):
            tot = tot + jnp.exp2(scores[blk, c : c + 128] - top)
        lse = top * math.log(2.0) + jnp.log(jnp.sum(tot, axis=1, keepdims=True))
        hi = lse.astype(BF16).astype(F32)
        mid = (lse - hi).astype(BF16).astype(F32)
        lane = lax.broadcasted_iota(jnp.int32, (block, 128), 1)
        split = jnp.where(lane == 0, hi, jnp.where(lane == 1, mid, jnp.where(lane == 2, lse - hi - mid, 0.0)))
        lse_col[blk, :] = split.astype(BF16)
        return m8

    m8 = lax.fori_loop(0, tok_count // block, score_rows, jnp.full((8, tok_count), NEG, F32))
    top = jnp.max(m8, axis=0, keepdims=True)

    def score_cols(i, s8):
        s = scores[pl.ds(pl.multiple_of(i * 64, 64), 64), :]
        return s8 + jnp.sum(jnp.exp2(s - top).reshape(8, 8, tok_count), axis=0)

    s8 = lax.fori_loop(0, tok_count // 64, score_cols, jnp.zeros((8, tok_count), F32))
    lse = top * math.log(2.0) + jnp.log(jnp.sum(s8, axis=0, keepdims=True))
    hi = lse.astype(BF16).astype(F32)
    mid = (lse - hi).astype(BF16).astype(F32)
    pieces = jnp.concatenate([hi, mid, lse - hi - mid, jnp.zeros((13, tok_count), F32)], axis=0)
    pick = jnp.where(
        lax.broadcasted_iota(jnp.int32, (width, width), 0) == lax.broadcasted_iota(jnp.int32, (width, width), 1), 1.0, 0.0
    ).astype(BF16)
    flip = (((1,), (1,)), ((), ()))
    table_r[0:width, :] = lax.dot_general(pick, right[...], flip, preferred_element_type=F32).astype(BF16)
    table_r[width : width + 16, :] = pieces.astype(BF16)
    table_l[0:width, :] = lax.dot_general(pick, left[...], flip, preferred_element_type=F32).astype(BF16)
    table_l[width : width + 16, :] = lax.dot_general(
        pick[0:16, :], lse_col[...], flip, preferred_element_type=F32
    ).astype(BF16)

    ml, mr = mleft[1 * home], mright[1 * home]
    index[0:1, :] = jnp.concatenate([ml[0:1, :], mr[1:2, :]], axis=1)
    index[1:2, :] = jnp.concatenate([ml[1:2, :], mr[0:1, :]], axis=1)

    @pl.loop(0, 2 * slots // 256)
    def _(g):
        lane = pl.ds(pl.multiple_of(g * 256, 256), 256)
        got = []
        for side, table in enumerate((table_l, table_r)):
            want = index[side : side + 1, lane]
            tt = lax.broadcasted_iota(jnp.int32, (256, 256), 0).astype(F32).astype(BF16)
            hot = []
            for kb in range(tok_count // 256):
                w = jnp.broadcast_to((want - kb * 256).astype(F32), (16, 256)).astype(BF16)
                w = jnp.concatenate([w] * 16, axis=0)
                hot.append(jnp.where(tt == w, jnp.ones_like(w), jnp.zeros_like(w)))
            got.append(jnp.dot(table[...], jnp.concatenate(hot, axis=0), preferred_element_type=F32))
        gl, gr = got
        pair = jnp.sum(gl[0:width] * gr[0:width], axis=0, keepdims=True) * scale
        lses = jnp.sum(gl[width : width + 8] + gr[width : width + 8], axis=0, keepdims=True)
        conf_both[0:1, lane] = 2.0 * pair - lses + 2.0 * math.log(tok_count)

    conf = conf_both[...]
    conf_out[0] = conf[:, 0:slots]
    conf_out[1] = conf[:, slots:]
    conf_r = remote(conf_out.at[1], conf_in.at[home], 9 - home, at(near, home * core + (1 - home) * (1 - core)))
    conf_l = remote(conf_out.at[0], conf_in.at[0], 10, far_other)
    conf_w0 = remote(conf_out.at[1], conf_in.at[0], 9, near_other)
    conf_w1 = remote(conf_out.at[1], conf_in.at[1], 8, near_same)
    conf_r.start()

    @pl.when(home == 0)
    def _():
        conf_l.start()

    def refine(rnd):
        low8 = req_in[rnd, 0:1, :] - 2
        goal = []
        for r in range(5):
            t = r - low8 + 50
            goal.append(jnp.broadcast_to(low8 + t - 5 * ((t * 205) >> 10), (8, slots)))
        xmid = jnp.broadcast_to(req_in[rnd, 1:2, :], (8, slots))
        iota = lax.broadcasted_iota(jnp.int32, (8, slots), 0)
        unit = (width ** -0.5) * math.log2(math.e)

        def strip(xt, m8):
            strip_map = mapb[:, pl.ds(pl.multiple_of(xt * 16, 16), 16), :].reshape(fine_h * 16, width)
            parts = []
            for half in range(slots // 256):
                cols = slice(half * 256, half * 256 + 256)
                h = lax.dot_general(
                    strip_map, q_in[rnd, cols, :], (((1,), (1,)), ((), ())), preferred_element_type=F32
                )
                best = m8[:, cols]
                sums = [[None, None] for _ in range(5)]
                for r in range(5):
                    for k in range(2):
                        sums[r][k] = jnp.zeros((8, 256), F32)
                for yy in range(fine_h):
                    r = yy % 5
                    hit = goal[r][:, cols] == yy
                    for k in range(2):
                        sums[r][k] = jnp.where(hit, h[yy * 16 + k * 8 : yy * 16 + k * 8 + 8, :], sums[r][k])
                for k in range(2):
                    dx = iota[:, cols] + (xt * 16 + k * 8) - xmid[:, cols]
                    inside = jnp.abs(dx) <= 2
                    for r in range(5):
                        v = jnp.where(inside, sums[r][k] * unit, NEG)
                        best = jnp.maximum(best, v)
                        acc[r, pl.ds(pl.multiple_of(xt * 16 + k * 8, 8), 8), cols] = v
                parts.append(best)
            return jnp.concatenate(parts, axis=1)

        m8 = lax.fori_loop(0, fine_w // 16, strip, jnp.full((8, slots), NEG, F32))
        x1 = req_in[rnd, 1:2, :]
        missing = jnp.maximum(2 - x1, 0) + jnp.maximum(x1 - (fine_w - 3), 0)
        top = jnp.max(m8, axis=0, keepdims=True)
        top = jnp.where(missing > 0, jnp.maximum(top, 0.0), top)
        zero = jnp.where(missing > 0, jnp.exp2(-jnp.maximum(top, 0.0)), 0.0) * 5.0
        gone = jnp.where(x1 == 0, -3.0, 0.0) + jnp.where(x1 == 1, -2.0, 0.0)
        gone = gone + jnp.where(x1 == fine_w - 1, 3.0, 0.0) + jnp.where(x1 == fine_w - 2, 2.0, 0.0)
        for jt in range(slots // 128):
            lane = slice(jt * 128, jt * 128 + 128)
            topb = jnp.broadcast_to(top[:, lane], (8, 128))
            z = [jnp.zeros((8, 128), F32) for _ in range(5)]
            sx = jnp.zeros((8, 128), F32)
            dx = (iota[:, lane] - xmid[:, lane]).astype(F32)
            for xt in range(fine_w // 8):
                es = [jnp.exp2(acc[r, xt * 8 : xt * 8 + 8, lane] - topb) for r in range(5)]
                z = [a + e for a, e in zip(z, es)]
                sx = sx + (es[0] + es[1] + es[2] + es[3] + es[4]) * (dx + (8.0 * xt))
            sy = jnp.zeros((8, 128), F32)
            for r in range(5):
                sy = sy + z[r] * (goal[r][:, lane] - low8[:, lane] - 2).astype(F32)
            tot1 = jnp.sum(z[0] + z[1] + z[2] + z[3] + z[4], axis=0, keepdims=True)
            sx1 = jnp.sum(sx, axis=0, keepdims=True)
            sy1 = jnp.sum(sy, axis=0, keepdims=True)
            tot1 = tot1 + zero[:, lane] * missing[:, lane].astype(F32)
            sx1 = sx1 + zero[:, lane] * gone[:, lane]
            off_out[rnd, 0:1, lane] = sx1 / tot1
            off_out[rnd, 1:2, lane] = sy1 / tot1

    off_cps = []
    for rnd in range(2):
        q_cps[2 * rnd].wait_recv()
        q_cps[2 * rnd + 1].wait_recv()
        refine(rnd)
        cp = remote(off_out.at[rnd], off_in.at[rnd], 11 + rnd, opp_same if rnd == 0 else near_same)
        cp.start()
        off_cps.append(cp)

    for rnd in range(2):
        off_cps[rnd].wait_recv()
        res_ref[2 * rnd + 2 : 2 * rnd + 4, :] = off_in[rnd]

    @pl.when(home == 1)
    def _():
        conf_l.wait_recv()
        conf_in[1] = conf_out[0]

    @pl.when(home == 0)
    def _():
        conf_w0.wait_recv()
        conf_w1.wait_recv()

    for rnd in range(2):
        res_ref[rnd : rnd + 1, :] = conf_in[rnd]

    for cp in q_cps + off_cps + [conf_r]:
        cp.wait_send()

    @pl.when(home == 1)
    def _():
        mat_a.wait_send()
        mat_f.wait_send()
        tok_f.wait_send()

    @pl.when(home == 0)
    def _():
        mat_b.wait_send()
        conf_l.wait_send()


def finish(res_ref, cnt_ref, conf_ref, off_ref):
    for rnd in range(2):
        valid = lax.broadcasted_iota(jnp.int32, (2, res_ref.shape[1]), 1) < cnt_ref[0, rnd]
        conf_ref[0, rnd : rnd + 1, :] = jnp.where(valid[0:1, :], res_ref[rnd : rnd + 1, :], 0.0)
        off_ref[0, rnd] = jnp.where(valid, res_ref[2 * rnd + 2 : 2 * rnd + 4, :], 0.0)


def solution(mesh):
    devices = mesh.size

    def body(tokens, fine_map, matches, subcells, counts):
        tok_count, width = tokens.shape
        fine_h, fine_w, _ = fine_map.shape
        points = fine_h * fine_w
        slots = matches.shape[3]
        whole = pl.BlockSpec(memory_space=pltpu.VMEM)
        vmem = pltpu.VMEM
        raw = pl.pallas_call(
            lambda *refs: kernel(devices, *refs),
            name="match_refine",
            out_shape=jax.ShapeDtypeStruct((8, slots), F32),
            in_specs=[pl.BlockSpec(memory_space=pltpu.HBM)] * 4,
            out_specs=whole,
            scratch_shapes=[
                vmem((fine_h, fine_w, width), BF16),
                vmem((points, width), F32),
                vmem((tok_count, width), BF16),
                vmem((tok_count, width), BF16),
                vmem((2, 2, slots), jnp.int32),
                vmem((2, 2, slots), jnp.int32),
                vmem((2, 2, slots), jnp.int32),
                vmem((2, 2, slots), jnp.int32),
                vmem((2, 1, slots), jnp.int32),
                pltpu.SMEM((1, slots), jnp.int32),
                pltpu.SMEM((1, slots), jnp.int32),
                vmem((2, 2, slots), jnp.int32),
                vmem((2, 2, slots), jnp.int32),
                vmem((slots, width), F32),
                vmem((2, slots, width), BF16),
                vmem((2, slots, width), BF16),
                vmem((5, fine_w, slots), F32),
                vmem((tok_count, tok_count), F32),
                vmem((tok_count, 128), BF16),
                vmem((width + 16, tok_count), BF16),
                vmem((width + 16, tok_count), BF16),
                vmem((2, 2 * slots), jnp.int32),
                vmem((1, 2 * slots), F32),
                vmem((2, 2, slots), F32),
                vmem((2, 2, slots), F32),
                vmem((2, 1, slots), F32),
                vmem((2, 1, slots), F32),
                pltpu.SemaphoreType.DMA((4,)),
                pltpu.SemaphoreType.DMA((13,)),
                pltpu.SemaphoreType.DMA((13,)),
            ],
            compiler_params=pltpu.CompilerParams(
                collective_id=0, has_side_effects=True, vmem_limit_bytes=60 * 1024 * 1024
            ),
        )(tokens, fine_map, matches[0], subcells[0])
        return pl.pallas_call(
            finish,
            name="finish",
            out_shape=(
                jax.ShapeDtypeStruct((1, 2, slots), F32),
                jax.ShapeDtypeStruct((1, 2, 2, slots), F32),
            ),
            in_specs=[whole, pl.BlockSpec(memory_space=pltpu.SMEM)],
            out_specs=(whole, whole),
        )(raw, counts)

    return jax.shard_map(
        body,
        mesh=mesh,
        in_specs=(
            P("frame", None),
            P("frame", None, None),
            P("frame", None, None, None),
            P("frame", None, None, None),
            P("frame", None),
        ),
        out_specs=(P("frame", None, None), P("frame", None, None, None)),
        check_vma=False,
    )
```

time: 71.6 us -> 49.2 us (0.69)
  Pallas kernels: 68.2 us -> 48.3 us
  local copies, waits for them, and re-layouts: 2.56 us -> 0 us
    pallas_call x1, Pallas kernels: 68.2 us -> 46.9 us  [body(): pl.pallas_call(lambda *refs: kernel(devices, *refs), name='match_refine',...]
    unnamed x2 -> x0, local copies, waits for them, and re-layouts: 2.56 us -> none
    pallas_call x0 -> x1, Pallas kernels: none -> 1.41 us  [body(): pl.pallas_call(finish, name='finish', out_shape=(jax.ShapeDtypeStruct((1,...]
where the time goes in v2:
time: 49.2 us; the launch traced here: 49 us
  Pallas kernels  48.3 us (98%)
  between operations  0.64 us (1%)
    pallas_call x1, Pallas kernels, body(): pl.pallas_call(lambda *refs: kernel(devices, *refs), name='match_refine',...  46.9 us
    pallas_call x1, Pallas kernels, body(): pl.pallas_call(finish, name='finish', out_shape=(jax.ShapeDtypeStruct((1,...  1.41 us

profile of v2, /device:TPU:1, one launch (start us, length us, event | category | flops | bytes accessed | tf_op | source)
XLA Modules:
  0.0 49.0 jit_solution(12765296814881499966)
XLA Ops:
  0.6 46.9 %match_refine.1.res_ref = f32[8,512]{1,0:T(8,128)} custom-call(bf16[1536,128]{1,0:T(8,128)(2,1)} %refs_0_.1, bf16[48,128,128]{2,1,0:T(8,128)(2,1)} %refs_1_.1, s32[2,2,512]{2,1,0:T(2,128)} %bitcast.2, s32[2,2,512]{2,1,0:T(2,128)} %bitcast.3), custom_call_target="tpu_custom_call" | custom-call | tf_op jit(solution)/shard_map/match_refine/pallas_call | solution.py:354
  47.5 1.4 %finish.1 = (f32[1,2,512]{2,1,0:T(2,128)}, f32[1,2,2,512]{3,2,1,0:T(2,128)}) custom-call(f32[8,512]{1,0:T(8,128)} %match_refine.1.res_ref, s32[1,2]{1,0:T(1,128)} %cnt_ref.1), custom_call_target="tpu_custom_call" | custom-call | tf_op jit(solution)/shard_map/finish/pallas_call | solution.py:396

commit v3 on v2

--- a/solution.py
+++ b/solution.py
@@ -16,7 +16,7 @@
 
 def kernel(
     devices, tok_hbm, map_hbm, mat_hbm, sub_hbm, res_ref,
-    mapb, mapf, left, right, mleft, mright, mat, sub, pvec, psm0, psm1, req_out, req_in, qf, q_out, q_in,
+    mapb, mapf, left, right, mleft, mright, mat, sub, pvec, psm0, psm1, req_out, req_in, qf, q_out, q_in, q_two,
     acc, scores, lse_col, table_l, table_r, index, conf_both,
     off_out, off_in, conf_out, conf_in, lsem, ssem, rsem,
 ):
@@ -114,20 +114,11 @@
 
         q_out[rnd] = qf[...].astype(BF16)
 
-    @pl.when(home == 1)
-    def _():
-        tok_a.wait_send()
-
-    @pl.when(home == 0)
-    def _():
-        tok_b.wait_send()
-
     q_cps = []
     for rnd in range(2):
         dev = opp_same if rnd == 0 else near_same
-        for cp in (remote(req_out.at[rnd], req_in.at[rnd], 4 + rnd, dev), remote(q_out.at[rnd], q_in.at[rnd], 6 + rnd, dev)):
-            cp.start()
-            q_cps.append(cp)
+        q_cps.append(remote(req_out.at[rnd], req_in.at[rnd], 4 + rnd, dev))
+        q_cps.append(remote(q_out.at[rnd], q_in.at[rnd], 6 + rnd, dev))
 
     @pl.when(home == 1)
     def _():
@@ -135,6 +126,10 @@
         tok_b.wait_recv()
         mat_f.start()
         tok_f.start()
+        q_cps[0].start()
+        q_cps[1].start()
+        q_cps[2].start()
+        q_cps[3].start()
         own_cp.wait()
         mleft[...] = mat[...]
 
@@ -142,6 +137,10 @@
     def _():
         mat_a.wait_recv()
         tok_a.wait_recv()
+        q_cps[0].start()
+        q_cps[1].start()
+        q_cps[2].start()
+        q_cps[3].start()
         mat_f.wait_recv()
         tok_f.wait_recv()
 
@@ -227,7 +226,14 @@
         conf_l.start()
 
     def refine(rnd):
-        low8 = req_in[rnd, 0:1, :] - 2
+        upper = jnp.where(req_in[rnd, 0:1, :] >= fine_h // 2, 1, 0)
+        flag = jnp.transpose(jnp.broadcast_to(upper.astype(F32), (width, slots)))
+        q = q_in[rnd].astype(F32)
+        q_two[:, 0:width] = jnp.where(flag > 0.5, 0.0, q).astype(BF16)
+        q_two[:, width:] = jnp.where(flag > 0.5, q, 0.0).astype(BF16)
+        shift = fine_h // 2 - 2
+        tall = fine_h - shift
+        low8 = req_in[rnd, 0:1, :] - 2 - shift * upper
         goal = []
         for r in range(5):
             t = r - low8 + 50
@@ -237,19 +243,22 @@
         unit = (width ** -0.5) * math.log2(math.e)
 
         def strip(xt, m8):
-            strip_map = mapb[:, pl.ds(pl.multiple_of(xt * 16, 16), 16), :].reshape(fine_h * 16, width)
+            cut = pl.ds(pl.multiple_of(xt * 16, 16), 16)
+            strip_map = jnp.concatenate(
+                [mapb[0:tall, cut, :].reshape(tall * 16, width), mapb[shift:, cut, :].reshape(tall * 16, width)], axis=1
+            )
             parts = []
             for half in range(slots // 256):
                 cols = slice(half * 256, half * 256 + 256)
                 h = lax.dot_general(
-                    strip_map, q_in[rnd, cols, :], (((1,), (1,)), ((), ())), preferred_element_type=F32
+                    strip_map, q_two[cols, :], (((1,), (1,)), ((), ())), preferred_element_type=F32
                 )
                 best = m8[:, cols]
                 sums = [[None, None] for _ in range(5)]
                 for r in range(5):
                     for k in range(2):
                         sums[r][k] = jnp.zeros((8, 256), F32)
-                for yy in range(fine_h):
+                for yy in range(tall):
                     r = yy % 5
                     hit = goal[r][:, cols] == yy
                     for k in range(2):
@@ -325,12 +334,14 @@
     @pl.when(home == 1)
     def _():
         mat_a.wait_send()
+        tok_a.wait_send()
         mat_f.wait_send()
         tok_f.wait_send()
 
     @pl.when(home == 0)
     def _():
         mat_b.wait_send()
+        tok_b.wait_send()
         conf_l.wait_send()
 
 
@@ -374,6 +385,7 @@
                 vmem((slots, width), F32),
                 vmem((2, slots, width), BF16),
                 vmem((2, slots, width), BF16),
+                vmem((slots, 2 * width), BF16),
                 vmem((5, fine_w, slots), F32),
                 vmem((tok_count, tok_count), F32),
                 vmem((tok_count, 128), BF16),

time: 49.2 us -> 47.4 us (0.963)
  Pallas kernels: 48.3 us -> 46.5 us
    pallas_call x1, Pallas kernels: 46.9 us -> 45.1 us  [body(): pl.pallas_call(lambda *refs: kernel(devices, *refs), name='match_refine',...]
where the time goes in v3:
time: 47.4 us; the launch traced here: 47.1 us
  Pallas kernels  46.5 us (98%)
  between operations  0.64 us (1%)
    pallas_call x1, Pallas kernels, body(): pl.pallas_call(lambda *refs: kernel(devices, *refs), name='match_refine',...  45.1 us
    pallas_call x1, Pallas kernels, body(): pl.pallas_call(finish, name='finish', out_shape=(jax.ShapeDtypeStruct((1,...  1.41 us

profile of v3, /device:TPU:1, one launch (start us, length us, event | category | flops | bytes accessed | tf_op | source)
XLA Modules:
  0.0 47.1 jit_solution(12474296848425638152)
XLA Ops:
  0.6 45.1 %match_refine.1.res_ref = f32[8,512]{1,0:T(8,128)} custom-call(bf16[1536,128]{1,0:T(8,128)(2,1)} %refs_0_.1, bf16[48,128,128]{2,1,0:T(8,128)(2,1)} %refs_1_.1, s32[2,2,512]{2,1,0:T(2,128)} %bitcast.2, s32[2,2,512]{2,1,0:T(2,128)} %bitcast.3), custom_call_target="tpu_custom_call" | custom-call | tf_op jit(solution)/shard_map/match_refine/pallas_call | solution.py:365
  45.7 1.4 %finish.1 = (f32[1,2,512]{2,1,0:T(2,128)}, f32[1,2,2,512]{3,2,1,0:T(2,128)}) custom-call(f32[8,512]{1,0:T(8,128)} %match_refine.1.res_ref, s32[1,2]{1,0:T(1,128)} %cnt_ref.1), custom_call_target="tpu_custom_call" | custom-call | tf_op jit(solution)/shard_map/finish/pallas_call | solution.py:408

commit v4 on v3

--- a/solution.py
+++ b/solution.py
@@ -273,7 +273,7 @@
                 parts.append(best)
             return jnp.concatenate(parts, axis=1)
 
-        m8 = lax.fori_loop(0, fine_w // 16, strip, jnp.full((8, slots), NEG, F32))
+        m8 = lax.fori_loop(0, fine_w // 16, strip, jnp.full((8, slots), NEG, F32), unroll=2)
         x1 = req_in[rnd, 1:2, :]
         missing = jnp.maximum(2 - x1, 0) + jnp.maximum(x1 - (fine_w - 3), 0)
         top = jnp.max(m8, axis=0, keepdims=True)

time: 47.4 us -> 45.7 us (0.964)
  Pallas kernels: 46.5 us -> 44.9 us
    pallas_call x1, Pallas kernels: 45.1 us -> 43.5 us  [body(): pl.pallas_call(lambda *refs: kernel(devices, *refs), name='match_refine',...]
where the time goes in v4:
time: 45.7 us; the launch traced here: 45.5 us
  Pallas kernels  44.9 us (98%)
  between operations  0.64 us (1%)
    pallas_call x1, Pallas kernels, body(): pl.pallas_call(lambda *refs: kernel(devices, *refs), name='match_refine',...  43.5 us
    pallas_call x1, Pallas kernels, body(): pl.pallas_call(finish, name='finish', out_shape=(jax.ShapeDtypeStruct((1,...  1.41 us

profile of v4, /device:TPU:1, one launch (start us, length us, event | category | flops | bytes accessed | tf_op | source)
XLA Modules:
  0.0 45.5 jit_solution(5019298377198034720)
XLA Ops:
  0.6 43.5 %match_refine.1.res_ref = f32[8,512]{1,0:T(8,128)} custom-call(bf16[1536,128]{1,0:T(8,128)(2,1)} %refs_0_.1, bf16[48,128,128]{2,1,0:T(8,128)(2,1)} %refs_1_.1, s32[2,2,512]{2,1,0:T(2,128)} %bitcast.2, s32[2,2,512]{2,1,0:T(2,128)} %bitcast.3), custom_call_target="tpu_custom_call" | custom-call | tf_op jit(solution)/shard_map/match_refine/pallas_call | solution.py:365
  44.1 1.4 %finish.1 = (f32[1,2,512]{2,1,0:T(2,128)}, f32[1,2,2,512]{3,2,1,0:T(2,128)}) custom-call(f32[8,512]{1,0:T(8,128)} %match_refine.1.res_ref, s32[1,2]{1,0:T(1,128)} %cnt_ref.1), custom_call_target="tpu_custom_call" | custom-call | tf_op jit(solution)/shard_map/finish/pallas_call | solution.py:408
